TPU v7x, 32 devices: a whole 2x2x4 slice. The times are simulated.
32 devices in a mesh: ctx: 16 (over z, x, core), head: 2 (over y).
Axes of the slice: x: 2, y: 2, z: 4, core: 2. Of those that a mesh axis runs over, the one named last changes fastest.
Arguments:
- teacher_queries: bfloat16 [8192, 4096], P('ctx', 'head'), may hold values from -13.5 to 13.5
- teacher_keys: bfloat16 [8192, 1024], P('ctx', 'head'), may hold values from -6 to 6
- query_projection: float32 [32, 128, 128], P('head'), may hold values from -0.5 to 0.5
- key_projection: float32 [8, 384, 128], P('head'), may hold values from -0.3125 to 0.3125
- block_offsets: int32 [128, 24], P('ctx'), may hold values from 0 to 24, as said below
- valid_counts: int32 [128], P('ctx'), may hold values from 1 to 24, as said below
Outputs:
- query_gradient: float32 [32, 128, 128], P('head')
- key_gradient: float32 [8, 384, 128], P('head')
- mean_divergence: float32 [], replicated
Inputs may be any that keep to these rules, and one draw needn't show every extreme that they name: `block_offsets`: each row holds distinct offsets, the first of them 0 (a block's own diagonal block); the largest offset is reached in every draw. `valid_counts`: both ends are reached in every draw.
All inputs are finite; a program needn't handle non-finite values.
Results may differ from a plain program's by a relative error of at most 0.0003.
Values may be sent and summed in bfloat16 or wider, within the bound.
A program may use at most 64 MiB of HBM per device.

v0:
```python
import functools
import math

import jax
import jax.numpy as jnp
from jax import lax
from jax.experimental import pallas as pl
from jax.experimental.pallas import tpu as pltpu
from jax.sharding import PartitionSpec as P

HEAD_DIM = 128
BLOCK = 64
REACH = 4
PIECES = 2
MESH = pl.DeviceIdType.MESH
F32 = jnp.float32
BF16 = jnp.bfloat16
LOW = -3.0e38
NT = (((1,), (1,)), ((), ()))
NN = (((1,), (0,)), ((), ()))
TN = (((0,), (0,)), ((), ()))


def exact(a, b, dims):
    return lax.dot_general(
        a, b, dims, precision=lax.Precision.HIGHEST, preferred_element_type=F32
    )


def halves(a):
    high = a.astype(BF16)
    return high, (a - high.astype(F32)).astype(BF16)


def dot3(a, b, dims):
    ah, al = halves(a)
    bh, bl = halves(b)
    one = functools.partial(
        lax.dot_general, dimension_numbers=dims, preferred_element_type=F32
    )
    return one(ah, bh) + (one(ah, bl) + one(al, bh))


def flipped(me, mask):
    out = me
    bit = 0
    while mask >> bit:
        if (mask >> bit) & 1:
            size = 1 << bit
            out = out + size - 2 * size * ((me // size) % 2)
        bit += 1
    return out


class Spread:
    def __init__(self, me, count, buf, send, recv):
        self.me, self.buf, self.send, self.recv = me, buf, send, recv
        self.bits = count.bit_length() - 1
        self.index = {}
        for bit in reversed(range(self.bits)):
            for high in range(1 << (self.bits - 1 - bit)):
                self.index[bit, high] = len(self.index)
        self.order = sorted(
            self.index, key=lambda key: (bin(key[1]).count("1"), -key[0])
        )
        self.done = 0

    def copy(self, bit, high):
        at = self.index[bit, high]
        slot = flipped(self.me, high << (bit + 1))
        return pltpu.make_async_remote_copy(
            src_ref=self.buf.at[slot],
            dst_ref=self.buf.at[slot],
            send_sem=self.send.at[at],
            recv_sem=self.recv.at[at],
            device_id={"ctx": flipped(self.me, 1 << bit)},
            device_id_type=MESH,
        )

    def start(self):
        for bit in reversed(range(self.bits)):
            self.copy(bit, 0).start()

    def forward(self, steps):
        for bit, high in self.order[self.done : self.done + steps]:
            self.copy(bit, high).wait_recv()
            held = (1 << bit) | (high << (bit + 1))
            for lower in reversed(range(bit)):
                self.copy(lower, held >> (lower + 1)).start()
        self.done += steps

    def finish(self):
        self.forward(len(self.order) - self.done)
        for bit, high in self.order:
            self.copy(bit, high).wait_send()


def kernel(
    count,
    heads_axis,
    q_in,
    k_ref,
    wq_in,
    wk_in,
    off_ref,
    cnt_ref,
    gq_out,
    gk_out,
    total_out,
    q_ref,
    wq_ref,
    wk_ref,
    load,
    win,
    early,
    late,
    peer,
    top,
    mass,
    mask,
    tmap,
    gq_own,
    gq_all,
    dq_all,
    gk_pad,
    dk_pad,
    win_send,
    win_recv,
    early_send,
    early_recv,
    late_send,
    late_recv,
    peer_send,
    peer_recv,
):
    loads = [
        pltpu.make_async_copy(src, dst, load.at[at])
        for at, (src, dst) in enumerate(((q_in, q_ref), (wq_in, wq_ref), (wk_in, wk_ref)))
    ]
    for copy in loads:
        copy.start()
    me = lax.axis_index("ctx")
    side = lax.axis_index("head")
    rows, width = q_ref.shape
    here = rows // BLOCK
    heads = width // HEAD_DIM
    kv = k_ref.shape[1] // HEAD_DIM
    group = heads // kv
    slots = off_ref.shape[1]
    blocks = REACH * here
    past = (REACH - 1) * here
    lanes = heads * here
    bits = count.bit_length() - 1
    span = group * BLOCK

    piece = rows // PIECES
    odd = lax.rem(me, 2) == 1

    def window_copy(kind, at, relay, step, target):
        base = (REACH - 3) * rows + at * piece
        dst = pl.ds((REACH - 1 - step) * rows + at * piece, piece)
        src = win.at[pl.ds(base, piece)] if relay else k_ref.at[pl.ds(at * piece, piece)]
        return pltpu.make_async_remote_copy(
            src_ref=src,
            dst_ref=win.at[dst],
            send_sem=win_send.at[kind, at],
            recv_sem=win_recv.at[step - 1, at],
            device_id={"ctx": lax.rem(target + count, count)},
            device_id_type=MESH,
        )

    def chip_copies(at):
        return (
            (me + 2 < count, window_copy(0, at, False, 2, me + 2)),
            (jnp.logical_not(odd), window_copy(1, at, False, 1, me + 1)),
        )

    def relay_copies(at):
        return (
            (odd & (me >= 2) & (me + 1 < count), window_copy(2, at, True, 3, me + 1)),
            (jnp.logical_not(odd) & (me >= 2), window_copy(3, at, True, 3, me + 1)),
            (odd & (me >= 2), window_copy(4, at, True, 1, me - 1)),
        )

    def arrived(step, at):
        return window_copy(0, at, False, step, me + 2).wait_recv()

    def relay(at):
        @pl.when(me >= 2)
        def _():
            arrived(2, at)

        for condition, copy in relay_copies(at):
            pl.when(condition)(copy.start)

    barrier = pltpu.get_barrier_semaphore()
    greeted = 0
    for step in range(1, REACH):
        for other in (lax.rem(me + step, count), lax.rem(me + count - step, count)):
            pl.semaphore_signal(
                barrier, inc=1, device_id={"ctx": other}, device_id_type=MESH
            )
            greeted += 1
    for bit in range(bits):
        pl.semaphore_signal(
            barrier, inc=1, device_id={"ctx": flipped(me, 1 << bit)}, device_id_type=MESH
        )
        greeted += 1
    for step in range(1, heads_axis):
        pl.semaphore_signal(
            barrier,
            inc=1,
            device_id={"head": lax.rem(side + step, heads_axis)},
            device_id_type=MESH,
        )
        greeted += 1
    pl.semaphore_wait(barrier, greeted)

    for at in range(PIECES):
        for condition, copy in chip_copies(at):
            pl.when(condition)(copy.start)

    for step in range(1, REACH):

        @pl.when(me < step)
        def _():
            win[(REACH - 1 - step) * rows : (REACH - step) * rows, :] = jnp.zeros(
                k_ref.shape, k_ref.dtype
            )

    loads[0].wait()

    pool_row = lax.broadcasted_iota(jnp.int32, (here, rows), 0)
    pool_col = lax.broadcasted_iota(jnp.int32, (here, rows), 1)
    pool = jnp.where(pool_col // BLOCK == pool_row, 1.0 / BLOCK, 0.0).astype(BF16)
    for h in range(heads):
        early[me, h * here : (h + 1) * here, :] = lax.dot_general(
            pool,
            q_ref[:, h * HEAD_DIM : (h + 1) * HEAD_DIM],
            NN,
            preferred_element_type=F32,
        )
    for g in range(kv):
        keys = k_ref[:, g * HEAD_DIM : (g + 1) * HEAD_DIM]
        split = keys.astype(F32).reshape(here, BLOCK, HEAD_DIM)
        mean = lax.dot_general(pool, keys, NN, preferred_element_type=F32)
        for part, value in enumerate((jnp.max(split, axis=1), jnp.min(split, axis=1), mean)):
            at = lanes + (g * 3 + part) * here
            early[me, at : at + here, :] = value
    first = Spread(me, count, early, early_send, early_recv)
    first.start()

    row_w = lax.broadcasted_iota(jnp.int32, (blocks, 128), 0)
    for j in range(here):
        back = past + j - row_w
        used = jnp.zeros((blocks, 128), F32)
        for c in range(slots):
            off = jnp.where(c < cnt_ref[0, j], off_ref[j, c], -1000)
            used = jnp.where(back == off, 1.0, used)
        mask[j] = jnp.where(row_w >= past - me * here, used, 0.0)

    log_scale = math.log2(math.e) / math.sqrt(HEAD_DIM)
    gap = lax.broadcasted_iota(jnp.int32, (BLOCK, span), 0) - (
        lax.broadcasted_iota(jnp.int32, (BLOCK, span), 1) % BLOCK
    )

    def section(base, keys_ref, key_row, diagonal):
        def one(j, carry):
            at = pl.ds(pl.multiple_of(j * BLOCK, BLOCK), BLOCK)
            for g in range(kv):
                queries = jnp.concatenate(
                    [
                        q_ref[at, (g * group + r) * HEAD_DIM : (g * group + r + 1) * HEAD_DIM]
                        for r in range(group)
                    ],
                    axis=0,
                )
                keys = keys_ref[pl.ds(key_row, rows), g * HEAD_DIM : (g + 1) * HEAD_DIM]
                scores = lax.dot_general(keys, queries, NT, preferred_element_type=F32)
                tops, sums = [], []
                for w in range(here):
                    part = scores[w * BLOCK : (w + 1) * BLOCK]
                    if diagonal:
                        part = jnp.where(gap <= jnp.where(j == w, 0, BLOCK), part, LOW)
                    high = jnp.max(part, axis=0, keepdims=True)
                    tops.append(high)
                    sums.append(
                        jnp.sum(jnp.exp2((part - high) * log_scale), axis=0, keepdims=True)
                    )
                top[j * kv + g, pl.ds(base, here), :] = jnp.concatenate(tops, axis=0)
                mass[j * kv + g, pl.ds(base, here), :] = jnp.concatenate(sums, axis=0)
            return carry

        lax.fori_loop(0, here, one, 0)

    def reached(step):
        @pl.when(me >= step)
        def _():
            for at in range(PIECES):
                arrived(step, at)

    def window_section(step):
        slot = REACH - 1 - step
        section(
            pl.multiple_of(slot * here, here), win, pl.multiple_of(slot * rows, rows), False
        )

    section(past, k_ref, 0, True)
    loads[1].wait()
    loads[2].wait()
    relay(0)
    own_gq = jnp.concatenate(
        [
            exact(early[me, h * here : (h + 1) * here, :], wq_ref[h], NN)
            for h in range(heads)
        ],
        axis=0,
    )
    gq_own[...] = own_gq
    for at in range(1, PIECES):
        relay(at)

    @pl.when(odd)
    def _():
        reached(1)

    window_section(jnp.where(odd, 1, 2))
    first.forward(min(3, len(first.order)))

    @pl.when(jnp.logical_not(odd))
    def _():
        reached(1)

    window_section(jnp.where(odd, 2, 1))
    first.forward(min(4, len(first.order) - first.done))
    reached(3)
    window_section(3)

    spread_row = lax.broadcasted_iota(jnp.int32, (span, 128), 0)
    spread_col = lax.broadcasted_iota(jnp.int32, (span, 128), 1)
    spread = jnp.where(spread_col == (spread_row // BLOCK) * here, 1.0 / BLOCK, 0.0).astype(BF16)
    tmap[...] = jnp.zeros(tmap.shape, F32)

    def combine(j, carry):
        used = mask[j] > 0.5
        used = jnp.concatenate([used] * (span // 128), axis=1)
        for g in range(kv):
            high = jnp.where(used, top[j * kv + g], LOW)
            best = jnp.max(high, axis=0, keepdims=True)
            share = jnp.where(used, mass[j * kv + g], 0.0) * jnp.exp2((high - best) * log_scale)
            share = share / jnp.sum(share, axis=0, keepdims=True)
            sh, sl = halves(share)
            mean = lax.dot_general(sh, spread, NN, preferred_element_type=F32)
            mean = mean + lax.dot_general(sl, spread, NN, preferred_element_type=F32)
            tmap[...] += pltpu.roll(mean, g * group * here + j, axis=1)
        return carry

    lax.fori_loop(0, here, combine, 0)

    first.forward(len(first.order) - first.done)

    gk_pad[:, :past, :] = jnp.zeros((kv, past, HEAD_DIM), F32)
    dk_pad[...] = jnp.zeros(dk_pad.shape, F32)

    def pooled_keys(g, part):
        at = lanes + (g * 3 + part) * here
        return early[:, at : at + here, :].reshape(count * here, HEAD_DIM)

    for g in range(kv):
        acc = exact(pooled_keys(g, 0), wk_ref[g, :HEAD_DIM, :], NN)
        for part in range(1, 3):
            acc = acc + exact(
                pooled_keys(g, part), wk_ref[g, part * HEAD_DIM : (part + 1) * HEAD_DIM, :], NN
            )
        gk_pad[g, past:, :] = acc

    def window_keys(s):
        at = pl.ds(pl.multiple_of(s * here, here), blocks)
        return jnp.concatenate([gk_pad[g, at, :] for g in range(kv)], axis=0)

    lane = lax.broadcasted_iota(jnp.int32, (blocks, lanes), 1)
    lane_group = lane // (group * here)
    full = exact(window_keys(me), gq_own[...], NT)
    logits = jnp.zeros((blocks, lanes), F32)
    used = jnp.zeros((blocks, lanes), F32)
    for g in range(kv):
        logits = jnp.where(lane_group == g, full[g * blocks : (g + 1) * blocks], logits)
    for j in range(here):
        used = jnp.where(lane % here == j, mask[j], used)
    used = used > 0.5
    logits = jnp.where(used, logits / math.sqrt(HEAD_DIM), LOW)
    logits = logits - jnp.max(logits, axis=0, keepdims=True)
    weights = jnp.where(used, jnp.exp(logits), 0.0)
    norm = jnp.sum(weights, axis=0, keepdims=True)
    log_gate = jnp.where(used, logits - jnp.log(norm), 0.0)
    teacher = jnp.where(used, tmap[...], 0.0)
    log_teacher = jnp.log(jnp.where(teacher > 0.0, teacher, 1.0))
    terms = teacher * (log_teacher - log_gate)
    block_total = count * here
    scale = 1.0 / (math.sqrt(block_total) * math.sqrt(HEAD_DIM))
    slope = jnp.sum(teacher, axis=0, keepdims=True) * (weights / norm) - teacher
    late[me, :blocks, :] = jnp.where(used, slope, 0.0) * scale
    part = terms[:8]
    for at in range(8, blocks, 8):
        part = part + terms[at : at + 8]
    late[me, blocks : blocks + 8, :] = part
    second = Spread(me, count, late, late_send, late_recv)
    second.start()

    for h in range(heads):
        pooled = early[:, h * here : (h + 1) * here, :].reshape(count * here, HEAD_DIM)
        gq_all[:, h * here : (h + 1) * here, :] = dot3(pooled, wq_ref[h], NN).reshape(
            count, here, HEAD_DIM
        )
        if h >= heads // 4:
            second.forward(min(1, len(second.order) - second.done))
    second.forward(len(second.order) - second.done)

    total = late[0, blocks : blocks + 8, :]
    for s in range(1, count):
        total = total + late[s, blocks : blocks + 8, :]
    peer[side] = total

    def peer_copy(step):
        return pltpu.make_async_remote_copy(
            src_ref=peer.at[side],
            dst_ref=peer.at[side],
            send_sem=peer_send.at[step - 1],
            recv_sem=peer_recv.at[step - 1],
            device_id={"head": lax.rem(side + step, heads_axis)},
            device_id_type=MESH,
        )

    for step in range(1, heads_axis):
        peer_copy(step).start()

    def backward(s, carry):
        slope = late[s, :blocks, :]
        banded = jnp.concatenate(
            [jnp.where(lane_group == g, slope, 0.0) for g in range(kv)], axis=0
        )
        dq_all[s] = dot3(banded, window_keys(s), TN)
        dk = dot3(banded, gq_all[s], NN)
        at = pl.ds(pl.multiple_of(s * here, here), blocks)
        for g in range(kv):
            dk_pad[g, at, :] += dk[g * blocks : (g + 1) * blocks]
        return carry

    lax.fori_loop(0, count, backward, 0)
    for h in range(heads):
        at = slice(h * here, (h + 1) * here)
        gq_out[h] = dot3(
            early[:, at, :].reshape(count * here, HEAD_DIM),
            dq_all[:, at, :].reshape(count * here, HEAD_DIM),
            TN,
        )
    for g in range(kv):
        for part in range(3):
            gk_out[g, part * HEAD_DIM : (part + 1) * HEAD_DIM, :] = dot3(
                pooled_keys(g, part), dk_pad[g, past:, :], TN
            )

    for step in range(1, heads_axis):
        peer_copy(step).wait_recv()
    total = peer[0]
    for step in range(1, heads_axis):
        total = total + peer[step]
    total = jnp.sum(jnp.sum(total, axis=0, keepdims=True), axis=1, keepdims=True)
    total_out[...] = total / (block_total * heads * heads_axis)
    for step in range(1, heads_axis):
        peer_copy(step).wait_send()
    first.finish()
    second.finish()
    for at in range(PIECES):
        for condition, copy in chip_copies(at) + relay_copies(at):
            pl.when(condition)(copy.wait_send)


def body(count, heads_axis, queries, keys, query_projection, key_projection, offsets, counts):
    rows, width = queries.shape
    here = rows // BLOCK
    heads = width // HEAD_DIM
    kv = keys.shape[1] // HEAD_DIM
    lanes = heads * here
    blocks = REACH * here
    past = blocks - here
    span = heads // kv * BLOCK
    early_rows = lanes + 3 * kv * here
    vmem = pl.BlockSpec(memory_space=pltpu.VMEM)
    hbm = pl.BlockSpec(memory_space=pl.ANY)
    smem = pl.BlockSpec(memory_space=pltpu.SMEM)
    dma = pltpu.SemaphoreType.DMA
    query_gradient, key_gradient, total = pl.pallas_call(
        functools.partial(kernel, count, heads_axis),
        out_shape=(
            jax.ShapeDtypeStruct(query_projection.shape, F32),
            jax.ShapeDtypeStruct(key_projection.shape, F32),
            jax.ShapeDtypeStruct((1, 1), F32),
        ),
        in_specs=[hbm, vmem, hbm, hbm] + [smem] * 2,
        out_specs=(vmem, vmem, vmem),
        scratch_shapes=[
            pltpu.VMEM(queries.shape, queries.dtype),
            pltpu.VMEM(query_projection.shape, F32),
            pltpu.VMEM(key_projection.shape, F32),
            dma((3,)),
            pltpu.VMEM((past * BLOCK, keys.shape[1]), keys.dtype),
            pltpu.VMEM((count, early_rows, HEAD_DIM), F32),
            pltpu.VMEM((count, blocks + 8, lanes), F32),
            pltpu.VMEM((heads_axis, 8, lanes), F32),
            pltpu.VMEM((here * kv, blocks, span), F32),
            pltpu.VMEM((here * kv, blocks, span), F32),
            pltpu.VMEM((here, blocks, 128), F32),
            pltpu.VMEM((blocks, lanes), F32),
            pltpu.VMEM((lanes, HEAD_DIM), F32),
            pltpu.VMEM((count, lanes, HEAD_DIM), F32),
            pltpu.VMEM((count, lanes, HEAD_DIM), F32),
            pltpu.VMEM((kv, past + count * here, HEAD_DIM), F32),
            pltpu.VMEM((kv, past + count * here, HEAD_DIM), F32),
            dma((5, PIECES)),
            dma((REACH - 1, PIECES)),
            dma((count - 1,)),
            dma((count - 1,)),
            dma((count - 1,)),
            dma((count - 1,)),
            dma((heads_axis,)),
            dma((heads_axis,)),
        ],
        compiler_params=pltpu.CompilerParams(
            collective_id=0, has_side_effects=True, vmem_limit_bytes=60 * 1024 * 1024
        ),
    )(queries, keys, query_projection, key_projection, offsets, counts.reshape(1, here))
    return query_gradient, key_gradient, total.reshape(())


def solution(mesh):
    placed = (
        P("ctx", "head"),
        P("ctx", "head"),
        P("head", None, None),
        P("head", None, None),
        P("ctx", None),
        P("ctx"),
    )
    return jax.shard_map(
        functools.partial(body, mesh.shape["ctx"], mesh.shape["head"]),
        mesh=mesh,
        in_specs=placed,
        out_specs=(P("head", None, None), P("head", None, None), P()),
        check_vma=False,
    )
```

profile of v0, /device:TPU:0, one launch (start us, length us, event | category | flops | bytes accessed | tf_op | source)
XLA Modules:
  0.0 64.1 jit_solution(16896729619291961950)
XLA Ops:
  0.6 58.4 %shard_map.85 = (f32[16,128,128]{2,1,0:T(8,128)}, f32[4,384,128]{2,1,0:T(8,128)}, f32[1,1]{1,0:T(1,128)}) custom-call(bf16[512,2048]{1,0:T(8,128)(2,1)} %q_in.1, bf16[512,512]{1,0:T(8,128)(2,1)} %k_ref.1, f32[16,128,128]{2,1,0:T(8,128)} %wq_in.1, f32[4,384,128]{2,1,0:T(8,128)} %wk_in.1, s32[8,24]{1,0:T(8,128)} %off_ref.1, s32[1,8]{1,0:T(1,128)} %bitcast.2), custom_call_target="tpu_custom_call" | custom-call | tf_op jit(solution)/shard_map/pallas_call | solution.py:493
  59.1 0.0 copy-start
  59.1 2.4 %copy.12 = f32[16,128,128]{2,1,0:T(8,128)} copy(f32[16,128,128]{2,1,0:T(8,128)} %get-tuple-element.12) | data formatting | bytes 2097152
  61.4 0.0 copy-done
  61.5 0.9 %copy.13 = f32[4,384,128]{2,1,0:T(8,128)} copy(f32[4,384,128]{2,1,0:T(8,128)S(1)} %copy-done) | data formatting | bytes 1572864
Async XLA Ops:
  59.1 2.4 %copy-start = (f32[4,384,128]{2,1,0:T(8,128)S(1)}, f32[4,384,128]{2,1,0:T(8,128)}, u32[]{:S(2)}) copy-start(f32[4,384,128]{2,1,0:T(8,128)} %get-tuple-element.13) | copy-start | bytes 2359300
where the time goes:
time: 65.1 us; the launch traced here: 64.1 us
  Pallas kernels  58.4 us (90%)
  local copies, waits for them, and re-layouts  3.25 us (5%)
  between operations  2.47 us (4%)
    pallas_call x1, Pallas kernels, body(): pl.pallas_call(functools.partial(kernel, count, heads_axis), out_shape=(j...  58.4 us
    unnamed x4, local copies, waits for them, and re-layouts  3.25 us

commit v1 on v0

--- a/solution.py
+++ b/solution.py
@@ -99,20 +99,23 @@
     count,
     heads_axis,
     q_in,
-    k_ref,
+    k_in,
     wq_in,
     wk_in,
+    off_in,
+    cnt_in,
+    early,
+    dq_all,
+    dk_pad,
+    total_out,
+    q_ref,
+    k_ref,
+    wq_ref,
+    wk_ref,
     off_ref,
     cnt_ref,
-    gq_out,
-    gk_out,
-    total_out,
-    q_ref,
-    wq_ref,
-    wk_ref,
     load,
     win,
-    early,
     late,
     peer,
     top,
@@ -121,9 +124,7 @@
     tmap,
     gq_own,
     gq_all,
-    dq_all,
     gk_pad,
-    dk_pad,
     win_send,
     win_recv,
     early_send,
@@ -135,7 +136,16 @@
 ):
     loads = [
         pltpu.make_async_copy(src, dst, load.at[at])
-        for at, (src, dst) in enumerate(((q_in, q_ref), (wq_in, wq_ref), (wk_in, wk_ref)))
+        for at, (src, dst) in enumerate(
+            (
+                (k_in, k_ref),
+                (q_in, q_ref),
+                (off_in, off_ref),
+                (cnt_in, cnt_ref),
+                (wq_in, wq_ref),
+                (wk_in, wk_ref),
+            )
+        )
     ]
     for copy in loads:
         copy.start()
@@ -159,7 +169,7 @@
     def window_copy(kind, at, relay, step, target):
         base = (REACH - 3) * rows + at * piece
         dst = pl.ds((REACH - 1 - step) * rows + at * piece, piece)
-        src = win.at[pl.ds(base, piece)] if relay else k_ref.at[pl.ds(at * piece, piece)]
+        src = win.at[pl.ds(base, piece)] if relay else k_in.at[pl.ds(at * piece, piece)]
         return pltpu.make_async_remote_copy(
             src_ref=src,
             dst_ref=win.at[dst],
@@ -228,7 +238,8 @@
                 k_ref.shape, k_ref.dtype
             )
 
-    loads[0].wait()
+    for copy in loads[:4]:
+        copy.wait()
 
     pool_row = lax.broadcasted_iota(jnp.int32, (here, rows), 0)
     pool_col = lax.broadcasted_iota(jnp.int32, (here, rows), 1)
@@ -306,8 +317,8 @@
         )
 
     section(past, k_ref, 0, True)
-    loads[1].wait()
-    loads[2].wait()
+    loads[4].wait()
+    loads[5].wait()
     relay(0)
     own_gq = jnp.concatenate(
         [
@@ -447,19 +458,6 @@
         return carry
 
     lax.fori_loop(0, count, backward, 0)
-    for h in range(heads):
-        at = slice(h * here, (h + 1) * here)
-        gq_out[h] = dot3(
-            early[:, at, :].reshape(count * here, HEAD_DIM),
-            dq_all[:, at, :].reshape(count * here, HEAD_DIM),
-            TN,
-        )
-    for g in range(kv):
-        for part in range(3):
-            gk_out[g, part * HEAD_DIM : (part + 1) * HEAD_DIM, :] = dot3(
-                pooled_keys(g, part), dk_pad[g, past:, :], TN
-            )
-
     for step in range(1, heads_axis):
         peer_copy(step).wait_recv()
     total = peer[0]
@@ -476,6 +474,35 @@
             pl.when(condition)(copy.wait_send)
 
 
+def finish(early, dq_all, dk_pad, gq_hbm, gk_hbm, gq_buf, gk_buf, sems):
+    count = early.shape[0]
+    heads, kv = gq_buf.shape[0], gk_buf.shape[0]
+    here = dq_all.shape[1] // heads
+    lanes = heads * here
+    past = dk_pad.shape[1] - count * here
+    copies = []
+
+    def put(src, dst):
+        copy = pltpu.make_async_copy(src, dst, sems.at[len(copies)])
+        copy.start()
+        copies.append(copy)
+
+    def rows(ref, at):
+        return ref[:, at : at + here, :].reshape(count * here, HEAD_DIM)
+
+    for h in range(heads):
+        gq_buf[h] = dot3(rows(early, h * here), rows(dq_all, h * here), TN)
+        put(gq_buf.at[h], gq_hbm.at[h])
+    for g in range(kv):
+        for part in range(3):
+            gk_buf[g, part * HEAD_DIM : (part + 1) * HEAD_DIM, :] = dot3(
+                rows(early, lanes + (g * 3 + part) * here), dk_pad[g, past:, :], TN
+            )
+        put(gk_buf.at[g], gk_hbm.at[g])
+    for copy in copies:
+        copy.wait()
+
+
 def body(count, heads_axis, queries, keys, query_projection, key_projection, offsets, counts):
     rows, width = queries.shape
     here = rows // BLOCK
@@ -487,25 +514,28 @@
     span = heads // kv * BLOCK
     early_rows = lanes + 3 * kv * here
     vmem = pl.BlockSpec(memory_space=pltpu.VMEM)
-    hbm = pl.BlockSpec(memory_space=pl.ANY)
-    smem = pl.BlockSpec(memory_space=pltpu.SMEM)
+    hbm = pl.BlockSpec(memory_space=pltpu.HBM)
     dma = pltpu.SemaphoreType.DMA
-    query_gradient, key_gradient, total = pl.pallas_call(
+    passed = 4 * HEAD_DIM * (count * (early_rows + lanes) + kv * (past + count * here))
+    early, dq_all, dk_pad, total = pl.pallas_call(
         functools.partial(kernel, count, heads_axis),
         out_shape=(
-            jax.ShapeDtypeStruct(query_projection.shape, F32),
-            jax.ShapeDtypeStruct(key_projection.shape, F32),
+            pltpu.VMEM((count, early_rows, HEAD_DIM), F32),
+            pltpu.VMEM((count, lanes, HEAD_DIM), F32),
+            pltpu.VMEM((kv, past + count * here, HEAD_DIM), F32),
             jax.ShapeDtypeStruct((1, 1), F32),
         ),
-        in_specs=[hbm, vmem, hbm, hbm] + [smem] * 2,
-        out_specs=(vmem, vmem, vmem),
+        in_specs=[hbm] * 6,
+        out_specs=(vmem, vmem, vmem, vmem),
         scratch_shapes=[
             pltpu.VMEM(queries.shape, queries.dtype),
+            pltpu.VMEM(keys.shape, keys.dtype),
             pltpu.VMEM(query_projection.shape, F32),
             pltpu.VMEM(key_projection.shape, F32),
-            dma((3,)),
+            pltpu.SMEM(offsets.shape, offsets.dtype),
+            pltpu.SMEM((1, here), counts.dtype),
+            dma((6,)),
             pltpu.VMEM((past * BLOCK, keys.shape[1]), keys.dtype),
-            pltpu.VMEM((count, early_rows, HEAD_DIM), F32),
             pltpu.VMEM((count, blocks + 8, lanes), F32),
             pltpu.VMEM((heads_axis, 8, lanes), F32),
             pltpu.VMEM((here * kv, blocks, span), F32),
@@ -514,8 +544,6 @@
             pltpu.VMEM((blocks, lanes), F32),
             pltpu.VMEM((lanes, HEAD_DIM), F32),
             pltpu.VMEM((count, lanes, HEAD_DIM), F32),
-            pltpu.VMEM((count, lanes, HEAD_DIM), F32),
-            pltpu.VMEM((kv, past + count * here, HEAD_DIM), F32),
             pltpu.VMEM((kv, past + count * here, HEAD_DIM), F32),
             dma((5, PIECES)),
             dma((REACH - 1, PIECES)),
@@ -527,9 +555,24 @@
             dma((heads_axis,)),
         ],
         compiler_params=pltpu.CompilerParams(
-            collective_id=0, has_side_effects=True, vmem_limit_bytes=60 * 1024 * 1024
+            collective_id=0, has_side_effects=True, vmem_limit_bytes=58 * 1024 * 1024 - passed
         ),
     )(queries, keys, query_projection, key_projection, offsets, counts.reshape(1, here))
+    query_gradient, key_gradient = pl.pallas_call(
+        finish,
+        out_shape=(
+            jax.ShapeDtypeStruct(query_projection.shape, F32),
+            jax.ShapeDtypeStruct(key_projection.shape, F32),
+        ),
+        in_specs=[vmem] * 3,
+        out_specs=(hbm, hbm),
+        scratch_shapes=[
+            pltpu.VMEM(query_projection.shape, F32),
+            pltpu.VMEM(key_projection.shape, F32),
+            dma((heads + kv,)),
+        ],
+        compiler_params=pltpu.CompilerParams(vmem_limit_bytes=16 * 1024 * 1024),
+    )(early, dq_all, dk_pad)
     return query_gradient, key_gradient, total.reshape(())
 
 

time: 65.1 us -> 61.2 us (0.940)
  local copies, waits for them, and re-layouts: 3.25 us -> 0 us
    unnamed x4 -> x0, local copies, waits for them, and re-layouts: 3.25 us -> none
    pallas_call x1 -> x2, Pallas kernels: 58.4 us -> 57.9 us  [the longest x1 56.1 us: body(): pl.pallas_call(functools.partial(kernel, count, heads_axis), out_shape=(p...]
where the time goes in v1:
time: 61.2 us; the launch traced here: 60.3 us
  Pallas kernels  57.9 us (95%)
  between operations  2.41 us (4%)
    pallas_call x1, Pallas kernels, body(): pl.pallas_call(functools.partial(kernel, count, heads_axis), out_shape=(p...  56.1 us
    pallas_call x1, Pallas kernels, body(): pl.pallas_call(finish, out_shape=(jax.ShapeDtypeStruct(query_projection.s...  1.79 us

profile of v1, /device:TPU:0, one launch (start us, length us, event | category | flops | bytes accessed | tf_op | source)
XLA Modules:
  0.0 60.3 jit_solution(7426406679084891110)
XLA Ops:
  0.6 56.1 %shard_map.85 = (f32[16,224,128]{2,1,0:T(8,128)S(1)}, f32[16,128,128]{2,1,0:T(8,128)S(1)}, f32[4,152,128]{2,1,0:T(8,128)S(1)}, f32[1,1]{1,0:T(1,128)}) custom-call(bf16[512,2048]{1,0:T(8,128)(2,1)} %q_in.1, bf16[512,512]{1,0:T(8,128)(2,1)} %k_in.1, f32[16,128,128]{2,1,0:T(8,128)} %wq_in.1, f32[4,384,128]{2,1,0:T(8,128)} %wk_in.1, s32[8,24]{1,0:T(8,128)} %off_in.1, ...), custom_call_target="tpu_custom_call" | custom-call | tf_op jit(solution)/shard_map/pallas_call | solution.py:520
  56.7 1.8 %shard_map.86 = (f32[16,128,128]{2,1,0:T(8,128)}, f32[4,384,128]{2,1,0:T(8,128)}) custom-call(f32[16,224,128]{2,1,0:T(8,128)S(1)} %get-tuple-element.9.early, f32[16,128,128]{2,1,0:T(8,128)S(1)} %get-tuple-element.10.dq_all, f32[4,152,128]{2,1,0:T(8,128)S(1)} %get-tuple-element.11.dk_pad), custom_call_target="tpu_custom_call" | custom-call | tf_op jit(solution)/shard_map/pallas_call | solution.py:561

commit v2 on v1

--- a/solution.py
+++ b/solution.py
@@ -63,7 +63,7 @@
         self.order = sorted(
             self.index, key=lambda key: (bin(key[1]).count("1"), -key[0])
         )
-        self.done = 0
+        self.whole = len(self.order)
 
     def copy(self, bit, high):
         at = self.index[bit, high]
@@ -81,16 +81,14 @@
         for bit in reversed(range(self.bits)):
             self.copy(bit, 0).start()
 
-    def forward(self, steps):
-        for bit, high in self.order[self.done : self.done + steps]:
+    def forward(self, begin, end):
+        for bit, high in self.order[begin:end]:
             self.copy(bit, high).wait_recv()
             held = (1 << bit) | (high << (bit + 1))
             for lower in reversed(range(bit)):
                 self.copy(lower, held >> (lower + 1)).start()
-        self.done += steps
 
     def finish(self):
-        self.forward(len(self.order) - self.done)
         for bit, high in self.order:
             self.copy(bit, high).wait_send()
 
@@ -163,45 +161,47 @@
     bits = count.bit_length() - 1
     span = group * BLOCK
 
-    piece = rows // PIECES
+    strip = kv // PIECES * HEAD_DIM
     odd = lax.rem(me, 2) == 1
-
-    def window_copy(kind, at, relay, step, target):
-        base = (REACH - 3) * rows + at * piece
-        dst = pl.ds((REACH - 1 - step) * rows + at * piece, piece)
-        src = win.at[pl.ds(base, piece)] if relay else k_in.at[pl.ds(at * piece, piece)]
+    even = jnp.logical_not(odd)
+    corner = lax.rem(me, 4)
+
+    def lanes_of(at):
+        if isinstance(at, int):
+            return slice(at * strip, (at + 1) * strip)
+        return pl.ds(pl.multiple_of(at * strip, strip), strip)
+
+    def slot_rows(step):
+        return pl.ds(pl.multiple_of((REACH - 1 - step) * rows, rows), rows)
+
+    def window_copy(kind, at, held, step, target):
+        if held:
+            src = win.at[slot_rows(held), lanes_of(at)]
+        else:
+            src = k_in.at[:, lanes_of(at)]
         return pltpu.make_async_remote_copy(
             src_ref=src,
-            dst_ref=win.at[dst],
+            dst_ref=win.at[slot_rows(step), lanes_of(at)],
             send_sem=win_send.at[kind, at],
             recv_sem=win_recv.at[step - 1, at],
             device_id={"ctx": lax.rem(target + count, count)},
             device_id_type=MESH,
         )
 
-    def chip_copies(at):
+    def direct_copies(at):
         return (
-            (me + 2 < count, window_copy(0, at, False, 2, me + 2)),
-            (jnp.logical_not(odd), window_copy(1, at, False, 1, me + 1)),
+            (even & (me + 2 < count), window_copy(0, at, 0, 2, me + 2)),
+            (even, window_copy(1, at, 0, 1, me + 1)),
+            ((corner == 1) & (me + 2 < count), window_copy(2, at, 0, 2, me + 2)),
+            (odd & (me + 3 < count), window_copy(3, at, 0, 3, me + 3)),
         )
 
     def relay_copies(at):
         return (
-            (odd & (me >= 2) & (me + 1 < count), window_copy(2, at, True, 3, me + 1)),
-            (jnp.logical_not(odd) & (me >= 2), window_copy(3, at, True, 3, me + 1)),
-            (odd & (me >= 2), window_copy(4, at, True, 1, me - 1)),
-        )
-
-    def arrived(step, at):
-        return window_copy(0, at, False, step, me + 2).wait_recv()
-
-    def relay(at):
-        @pl.when(me >= 2)
-        def _():
-            arrived(2, at)
-
-        for condition, copy in relay_copies(at):
-            pl.when(condition)(copy.start)
+            (2, even & (me >= 2), window_copy(4, at, 2, 3, me + 1)),
+            (2, odd & (me >= 2), window_copy(5, at, 2, 1, me - 1)),
+            (3, (corner == 2) & (me >= 3), window_copy(6, at, 3, 2, me - 1)),
+        )
 
     barrier = pltpu.get_barrier_semaphore()
     greeted = 0
@@ -227,7 +227,7 @@
     pl.semaphore_wait(barrier, greeted)
 
     for at in range(PIECES):
-        for condition, copy in chip_copies(at):
+        for condition, copy in direct_copies(at):
             pl.when(condition)(copy.start)
 
     for step in range(1, REACH):
@@ -259,7 +259,6 @@
             at = lanes + (g * 3 + part) * here
             early[me, at : at + here, :] = value
     first = Spread(me, count, early, early_send, early_recv)
-    first.start()
 
     row_w = lax.broadcasted_iota(jnp.int32, (blocks, 128), 0)
     for j in range(here):
@@ -275,51 +274,57 @@
         lax.broadcasted_iota(jnp.int32, (BLOCK, span), 1) % BLOCK
     )
 
-    def section(base, keys_ref, key_row, diagonal):
-        def one(j, carry):
-            at = pl.ds(pl.multiple_of(j * BLOCK, BLOCK), BLOCK)
-            for g in range(kv):
-                queries = jnp.concatenate(
-                    [
-                        q_ref[at, (g * group + r) * HEAD_DIM : (g * group + r + 1) * HEAD_DIM]
-                        for r in range(group)
-                    ],
-                    axis=0,
-                )
-                keys = keys_ref[pl.ds(key_row, rows), g * HEAD_DIM : (g + 1) * HEAD_DIM]
-                scores = lax.dot_general(keys, queries, NT, preferred_element_type=F32)
-                tops, sums = [], []
-                for w in range(here):
-                    part = scores[w * BLOCK : (w + 1) * BLOCK]
-                    if diagonal:
-                        part = jnp.where(gap <= jnp.where(j == w, 0, BLOCK), part, LOW)
-                    high = jnp.max(part, axis=0, keepdims=True)
-                    tops.append(high)
-                    sums.append(
-                        jnp.sum(jnp.exp2((part - high) * log_scale), axis=0, keepdims=True)
-                    )
-                top[j * kv + g, pl.ds(base, here), :] = jnp.concatenate(tops, axis=0)
-                mass[j * kv + g, pl.ds(base, here), :] = jnp.concatenate(sums, axis=0)
+    count_row = lax.broadcasted_iota(jnp.int32, (here, rows), 0)
+    count_col = lax.broadcasted_iota(jnp.int32, (here, rows), 1)
+    tally = jnp.where(count_col // BLOCK == count_row, 1.0, 0.0).astype(BF16)
+
+    def lane(at):
+        return pl.ds(pl.multiple_of(at * HEAD_DIM, HEAD_DIM), HEAD_DIM)
+
+    def scored(keys_ref, key_row, j, g, low, high):
+        here_rows = slice(j * BLOCK, (j + 1) * BLOCK)
+        queries = jnp.concatenate(
+            [q_ref[here_rows, lane(g * group + r)] for r in range(group)], axis=0
+        )
+        keys = keys_ref[pl.ds(key_row + low * BLOCK, (high - low) * BLOCK), lane(g)]
+        return lax.dot_general(keys, queries, NT, preferred_element_type=F32)
+
+    def weigh(scores, base, j, g, low, high, diagonal):
+        none = [jnp.zeros((1, span), F32)]
+        tops, sums = none * low, none * low
+        for w in range(low, high):
+            part = scores[(w - low) * BLOCK : (w - low + 1) * BLOCK]
+            if diagonal and w == j:
+                part = jnp.where(gap <= 0, part, LOW)
+            best = jnp.max(part, axis=0, keepdims=True)
+            tops.append(best)
+            power = jnp.exp2((part - best) * log_scale)
+            sums.append(jnp.sum(power, axis=0, keepdims=True))
+        tops += none * (here - high)
+        top[j * kv + g, pl.ds(base, here), :] = jnp.concatenate(tops, axis=0)
+        return sums
+
+    def keep(sums, base, j, g, low, high):
+        mass[j * kv + g, pl.ds(base, here), :] = jnp.concatenate(
+            sums + [jnp.zeros((1, span), F32)] * (here - high), axis=0
+        )
+
+    def section(keys_ref, key_row, base, first_g, last_g, bounds, diagonal=False):
+        def one(g, carry):
+            ahead = scored(keys_ref, key_row, 0, g, *bounds(0))
+            for j in range(here):
+                scores = ahead
+                if j + 1 < here:
+                    ahead = scored(keys_ref, key_row, j + 1, g, *bounds(j + 1))
+                sums = weigh(scores, base, j, g, *bounds(j), diagonal)
+                keep(sums, base, j, g, *bounds(j))
             return carry
 
-        lax.fori_loop(0, here, one, 0)
-
-    def reached(step):
-        @pl.when(me >= step)
-        def _():
-            for at in range(PIECES):
-                arrived(step, at)
-
-    def window_section(step):
-        slot = REACH - 1 - step
-        section(
-            pl.multiple_of(slot * here, here), win, pl.multiple_of(slot * rows, rows), False
-        )
-
-    section(past, k_ref, 0, True)
+        lax.fori_loop(first_g, last_g, one, 0)
+
+    section(k_ref, 0, past, 0, kv, lambda j: (0, j + 1), True)
     loads[4].wait()
     loads[5].wait()
-    relay(0)
     own_gq = jnp.concatenate(
         [
             exact(early[me, h * here : (h + 1) * here, :], wq_ref[h], NN)
@@ -328,24 +333,49 @@
         axis=0,
     )
     gq_own[...] = own_gq
-    for at in range(1, PIECES):
-        relay(at)
-
-    @pl.when(odd)
-    def _():
-        reached(1)
-
-    window_section(jnp.where(odd, 1, 2))
-    first.forward(min(3, len(first.order)))
-
-    @pl.when(jnp.logical_not(odd))
-    def _():
-        reached(1)
-
-    window_section(jnp.where(odd, 2, 1))
-    first.forward(min(4, len(first.order) - first.done))
-    reached(3)
-    window_section(3)
+
+    reached = [
+        sum(bin(high).count("1") <= ones for _, high in first.order) for ones in range(2)
+    ]
+
+    def piece(turn, carry):
+        plan = (
+            ((3, 0), (2, 0), (3, 1), (1, 0), (2, 1), (1, 1)),
+            ((1, 0), (1, 1), (2, 0), (3, 0), (2, 1), (3, 1)),
+        )
+        step, at = jnp.int32(0), jnp.int32(0)
+        for number, (evens, odds) in enumerate(zip(*plan)):
+            step = jnp.where(turn == number, jnp.where(odd, odds[0], evens[0]), step)
+            at = jnp.where(turn == number, jnp.where(odd, odds[1], evens[1]), at)
+
+        @pl.when(me >= step)
+        def _():
+            window_copy(0, at, 0, step, me + 2).wait_recv()
+
+        for want, condition, copy in relay_copies(at):
+            pl.when(condition & (step == want))(copy.start)
+
+        slot = REACH - 1 - step
+        key_row = pl.multiple_of(slot * rows, rows)
+        base = pl.multiple_of(slot * here, here)
+        each = kv // PIECES
+
+        @pl.when(step == REACH - 1)
+        def _():
+            section(win, key_row, base, at * each, at * each + each, lambda j: (j, here))
+
+        @pl.when(step < REACH - 1)
+        def _():
+            section(win, key_row, base, at * each, at * each + each, lambda j: (0, here))
+
+        @pl.when(turn == 1)
+        def _():
+            first.start()
+
+        return carry
+
+    lax.fori_loop(0, (REACH - 1) * PIECES, piece, 0)
+    first.forward(0, reached[0])
 
     spread_row = lax.broadcasted_iota(jnp.int32, (span, 128), 0)
     spread_col = lax.broadcasted_iota(jnp.int32, (span, 128), 1)
@@ -368,30 +398,34 @@
 
     lax.fori_loop(0, here, combine, 0)
 
-    first.forward(len(first.order) - first.done)
-
-    gk_pad[:, :past, :] = jnp.zeros((kv, past, HEAD_DIM), F32)
-    dk_pad[...] = jnp.zeros(dk_pad.shape, F32)
+    first.forward(reached[0], reached[1])
+    win_row = lax.broadcasted_iota(jnp.int32, (past, past * BLOCK), 0)
+    win_col = lax.broadcasted_iota(jnp.int32, (past, past * BLOCK), 1)
+    win_pool = jnp.where(win_col // BLOCK == win_row, 1.0 / BLOCK, 0.0).astype(BF16)
+    near = []
+    for g in range(kv):
+        keys = win[:, g * HEAD_DIM : (g + 1) * HEAD_DIM]
+        split = keys.astype(F32).reshape(past, BLOCK, HEAD_DIM)
+        mean = lax.dot_general(win_pool, keys, NN, preferred_element_type=F32)
+        acc = None
+        for part, value in enumerate((jnp.max(split, axis=1), jnp.min(split, axis=1), mean)):
+            at = lanes + (g * 3 + part) * here
+            value = jnp.concatenate([value, early[me, at : at + here, :]], axis=0)
+            term = exact(value, wk_ref[g, part * HEAD_DIM : (part + 1) * HEAD_DIM, :], NN)
+            acc = term if acc is None else acc + term
+        near.append(acc)
 
     def pooled_keys(g, part):
         at = lanes + (g * 3 + part) * here
         return early[:, at : at + here, :].reshape(count * here, HEAD_DIM)
 
-    for g in range(kv):
-        acc = exact(pooled_keys(g, 0), wk_ref[g, :HEAD_DIM, :], NN)
-        for part in range(1, 3):
-            acc = acc + exact(
-                pooled_keys(g, part), wk_ref[g, part * HEAD_DIM : (part + 1) * HEAD_DIM, :], NN
-            )
-        gk_pad[g, past:, :] = acc
-
     def window_keys(s):
         at = pl.ds(pl.multiple_of(s * here, here), blocks)
         return jnp.concatenate([gk_pad[g, at, :] for g in range(kv)], axis=0)
 
     lane = lax.broadcasted_iota(jnp.int32, (blocks, lanes), 1)
     lane_group = lane // (group * here)
-    full = exact(window_keys(me), gq_own[...], NT)
+    full = exact(jnp.concatenate(near, axis=0), gq_own[...], NT)
     logits = jnp.zeros((blocks, lanes), F32)
     used = jnp.zeros((blocks, lanes), F32)
     for g in range(kv):
@@ -418,14 +452,23 @@
     second = Spread(me, count, late, late_send, late_recv)
     second.start()
 
+    first.forward(reached[1], first.whole)
+    gk_pad[:, :past, :] = jnp.zeros((kv, past, HEAD_DIM), F32)
+    dk_pad[...] = jnp.zeros(dk_pad.shape, F32)
+    for g in range(kv):
+        acc = exact(pooled_keys(g, 0), wk_ref[g, :HEAD_DIM, :], NN)
+        for part in range(1, 3):
+            acc = acc + exact(
+                pooled_keys(g, part), wk_ref[g, part * HEAD_DIM : (part + 1) * HEAD_DIM, :], NN
+            )
+        gk_pad[g, past:, :] = acc
+
     for h in range(heads):
         pooled = early[:, h * here : (h + 1) * here, :].reshape(count * here, HEAD_DIM)
         gq_all[:, h * here : (h + 1) * here, :] = dot3(pooled, wq_ref[h], NN).reshape(
             count, here, HEAD_DIM
         )
-        if h >= heads // 4:
-            second.forward(min(1, len(second.order) - second.done))
-    second.forward(len(second.order) - second.done)
+        second.forward(h * second.whole // heads, (h + 1) * second.whole // heads)
 
     total = late[0, blocks : blocks + 8, :]
     for s in range(1, count):
@@ -470,7 +513,9 @@
     first.finish()
     second.finish()
     for at in range(PIECES):
-        for condition, copy in chip_copies(at) + relay_copies(at):
+        for condition, copy in direct_copies(at):
+            pl.when(condition)(copy.wait_send)
+        for _, condition, copy in relay_copies(at):
             pl.when(condition)(copy.wait_send)
 
 
@@ -545,7 +590,7 @@
             pltpu.VMEM((lanes, HEAD_DIM), F32),
             pltpu.VMEM((count, lanes, HEAD_DIM), F32),
             pltpu.VMEM((kv, past + count * here, HEAD_DIM), F32),
-            dma((5, PIECES)),
+            dma((7, PIECES)),
             dma((REACH - 1, PIECES)),
             dma((count - 1,)),
             dma((count - 1,)),

time: 61.2 us -> 58 us (0.948); the launches traced: 60.3 us -> 57.8 us
  Pallas kernels: 57.9 us -> 55.4 us
    pallas_call x1, Pallas kernels: 56.1 us -> 53.6 us  [body(): pl.pallas_call(functools.partial(kernel, count, heads_axis), out_shape=(p...]
where the time goes in v2:
time: 58 us; the launch traced here: 57.8 us
  Pallas kernels  55.4 us (96%)
  between operations  2.41 us (4%)
    pallas_call x1, Pallas kernels, body(): pl.pallas_call(functools.partial(kernel, count, heads_axis), out_shape=(p...  53.6 us
    pallas_call x1, Pallas kernels, body(): pl.pallas_call(finish, out_shape=(jax.ShapeDtypeStruct(query_projection.s...  1.79 us

profile of v2, /device:TPU:0, one launch (start us, length us, event | category | flops | bytes accessed | tf_op | source)
XLA Modules:
  0.0 57.8 jit_solution(10383244213223802552)
XLA Ops:
  0.6 53.6 %shard_map.85 = (f32[16,224,128]{2,1,0:T(8,128)S(1)}, f32[16,128,128]{2,1,0:T(8,128)S(1)}, f32[4,152,128]{2,1,0:T(8,128)S(1)}, f32[1,1]{1,0:T(1,128)}) custom-call(bf16[512,2048]{1,0:T(8,128)(2,1)} %q_in.1, bf16[512,512]{1,0:T(8,128)(2,1)} %k_in.1, f32[16,128,128]{2,1,0:T(8,128)} %wq_in.1, f32[4,384,128]{2,1,0:T(8,128)} %wk_in.1, s32[8,24]{1,0:T(8,128)} %off_in.1, ...), custom_call_target="tpu_custom_call" | custom-call | tf_op jit(solution)/shard_map/pallas_call | solution.py:565
  54.3 1.8 %shard_map.86 = (f32[16,128,128]{2,1,0:T(8,128)}, f32[4,384,128]{2,1,0:T(8,128)}) custom-call(f32[16,224,128]{2,1,0:T(8,128)S(1)} %get-tuple-element.9.early, f32[16,128,128]{2,1,0:T(8,128)S(1)} %get-tuple-element.10.dq_all, f32[4,152,128]{2,1,0:T(8,128)S(1)} %get-tuple-element.11.dk_pad), custom_call_target="tpu_custom_call" | custom-call | tf_op jit(solution)/shard_map/pallas_call | solution.py:606
